TPU v7x, 128 devices: a whole 4x4x4 slice. The times are simulated.
128 devices in a mesh: row: 8 (over y, core), col: 16 (over x, z).
Axes of the slice: x: 4, y: 4, z: 4, core: 2. Of those that a mesh axis runs over, the one named last changes fastest.
Arguments:
- descriptors: bfloat16 [16384, 1024], P(('row', 'col'))
- gradients: bfloat16 [3, 4, 16384, 1024], P(None, None, ('row', 'col'))
- sparse_panel: bfloat16 [512, 1024], P('col')
- sparse_trail: bfloat16 [2048, 1024], P('col')
- atom_counts: int32 [128, 8], P(('row', 'col')), may hold values from 1 to 16, 64 in all within a row
- owner_rows: int32 [128, 8], P(('row', 'col')), may hold values from 0 to 7, each once within a row
- neighbor_ids: int32 [1024, 16, 4], P(('row', 'col')), may hold values from 0 to 65519
Outputs:
- panel_factor: float32 [512, 512], replicated
- cross_factor: float32 [2048, 512], P('col')
- trail_residual: float32 [2048, 65536], P('col', 'row')
Inputs may be any that keep to these rules, and one draw needn't show every extreme that they name: `atom_counts`: the structures of one device's line hold 64 atoms together, and every line has a structure of 16 atoms. `owner_rows`: every device gives exactly one structure to each row group.
All inputs are finite; a program needn't handle non-finite values.
Results may differ from a plain program's by a relative error of at most 0.0043.
Values may be sent and summed in bfloat16 or wider, within the bound.
No kernel may reach another device: no remote copies, remote signals or barrier semaphores. Data moves between devices by JAX's collectives and lax.ppermute only.
A program may use at most 128 MiB of HBM per device.

v0:
```python
import jax
import jax.numpy as jnp
from jax import lax
from jax.sharding import PartitionSpec as P

ridge_value = 0.1


def slot_rows(environments, desc_here, slope_here, count_here, neighbor_here, owner_here):
    struct_count = count_here.shape[0]
    atom_slots = neighbor_here.shape[1]
    neighbor_count = neighbor_here.shape[2]
    env_count = environments.shape[0]
    correlation = lax.dot_general(
        environments, desc_here, (((1,), (1,)), ((), ())), preferred_element_type=jnp.float32
    )
    slope_dots = lax.dot_general(
        environments, slope_here, (((1,), (1,)), ((), ())), preferred_element_type=jnp.float32
    )
    slope_dots = slope_dots.reshape(env_count, 3, neighbor_count, struct_count, atom_slots)
    slot_index = jnp.arange(atom_slots, dtype=jnp.int32)
    live_mask = (slot_index[None, :] < count_here[:, None]).astype(jnp.float32)
    squares = (correlation * correlation).reshape(env_count, struct_count, atom_slots)
    energy = jnp.sum(squares * live_mask[None], axis=2) / count_here.astype(jnp.float32)[None, :]
    partner = neighbor_here % count_here[:, None, None]
    struct_index = jnp.arange(struct_count, dtype=jnp.int32)
    flat_index = (struct_index[:, None, None] * atom_slots + partner).reshape(-1)
    picked = jnp.take(correlation, flat_index, axis=1).reshape(
        env_count, struct_count, atom_slots, neighbor_count
    )
    picked = jnp.transpose(picked, (0, 3, 1, 2))
    forces = -2.0 * jnp.sum(picked[:, None] * slope_dots, axis=2) * live_mask[None, None]
    forces = jnp.transpose(forces, (0, 2, 3, 1)).reshape(env_count, struct_count, 3 * atom_slots)
    padding = jnp.zeros((env_count, struct_count, atom_slots - 1), jnp.float32)
    slot_values = jnp.concatenate([energy[:, :, None], forces, padding], axis=2).astype(
        jnp.bfloat16
    )
    chosen = (owner_here[None, :] == struct_index[:, None]).astype(jnp.int32)
    owner_order = jnp.sum(struct_index[None, :] * chosen, axis=1)
    return jnp.take(slot_values, owner_order, axis=1)


def factor_panel(gram_sum, cross_sum, total_rows):
    gram_matrix = gram_sum / total_rows + ridge_value * jnp.eye(
        gram_sum.shape[0], dtype=jnp.float32
    )
    lower_factor = jnp.linalg.cholesky(gram_matrix)
    coupling = lax.linalg.triangular_solve(
        lower_factor, cross_sum / total_rows, left_side=True, lower=True
    )
    weights = lax.linalg.triangular_solve(
        lower_factor, coupling, left_side=True, lower=True, transpose_a=True
    )
    return (lower_factor.T, coupling, weights)


def split_weights(weights):
    weight_high = weights.astype(jnp.bfloat16)
    held_high = lax.optimization_barrier(weight_high)
    weight_low = (weights - held_high.astype(jnp.float32)).astype(jnp.bfloat16)
    return (weight_high, weight_low)


def reduce_products(gram_part, cross_part):
    return lax.psum((gram_part, cross_part), ("row", "col"))


def contract_rows(left_side, right_side):
    return lax.dot_general(
        left_side, right_side, (((1,), (1,)), ((), ())), preferred_element_type=jnp.float32
    )


def contract_cols(left_side, right_side):
    return lax.dot_general(
        left_side, right_side, (((0,), (0,)), ((), ())), preferred_element_type=jnp.float32
    )


def arrange_direct(block_rows, row_count, col_count):
    env_width = block_rows.shape[0] // col_count
    slot_count = block_rows.shape[2]
    shaped = block_rows.reshape(col_count, env_width, row_count, slot_count)
    return jnp.transpose(shaped, (2, 0, 1, 3)).reshape(row_count * col_count, env_width, slot_count)


def restore_direct(block_rows, row_count, col_count):
    env_width = block_rows.shape[1]
    slot_count = block_rows.shape[2]
    shaped = block_rows.reshape(row_count, col_count, env_width, slot_count)
    return jnp.transpose(shaped, (2, 1, 0, 3)).reshape(
        env_width, row_count * col_count * slot_count
    )


def per_device(
    descriptors, gradients, sparse_panel, sparse_trail, atom_counts, owner_rows, neighbor_ids
):
    row_count = lax.axis_size("row")
    col_count = lax.axis_size("col")
    col_index = lax.axis_index("col")
    count_here = atom_counts[0]
    owner_here = owner_rows[0]
    slope_here = gradients.reshape(-1, gradients.shape[3])
    panel_width = sparse_panel.shape[0]
    trail_width = sparse_trail.shape[0]
    panel_total = panel_width * col_count
    trail_total = trail_width * col_count
    slot_count = 4 * neighbor_ids.shape[1]
    total_rows = row_count * row_count * col_count * slot_count
    own_envs = jnp.concatenate([sparse_panel, sparse_trail], axis=0)
    kernel_rows = slot_rows(
        lax.all_gather(own_envs, "col", axis=0, tiled=True),
        descriptors,
        slope_here,
        count_here,
        neighbor_ids,
        owner_here,
    )
    blocks = kernel_rows.reshape(col_count, panel_width + trail_width, row_count, slot_count)
    panel_rows = blocks[:, :panel_width].reshape(panel_total, row_count, slot_count)
    trail_rows = blocks[:, panel_width:].reshape(trail_total, row_count, slot_count)
    received = (
        lax.all_to_all(
            arrange_direct(panel_rows, row_count, col_count),
            ("row", "col"),
            split_axis=0,
            concat_axis=0,
            tiled=True,
        ),
        lax.all_to_all(
            arrange_direct(trail_rows, row_count, col_count),
            ("row", "col"),
            split_axis=0,
            concat_axis=0,
            tiled=True,
        ),
    )
    panel_own = restore_direct(received[0], row_count, col_count)
    trail_own = restore_direct(received[1], row_count, col_count)
    segment = lax.all_gather(panel_own, "col", axis=0, tiled=True)
    columns = jnp.concatenate(
        [contract_rows(segment, panel_own), contract_rows(segment, trail_own)], axis=1
    )
    gram_part = lax.dynamic_update_slice(
        jnp.zeros((panel_total, panel_total), jnp.float32),
        columns[:, :panel_width],
        (0, col_index * panel_width),
    )
    cross_part = lax.dynamic_update_slice(
        jnp.zeros((panel_total, trail_total), jnp.float32),
        columns[:, panel_width:],
        (0, col_index * trail_width),
    )
    gram_sum, cross_sum = reduce_products(gram_part, cross_part)
    panel_factor, coupling, weights = factor_panel(gram_sum, cross_sum, total_rows)
    coupling_own = lax.dynamic_slice_in_dim(coupling, col_index * trail_width, trail_width, 1)
    weights_own = lax.dynamic_slice_in_dim(weights, col_index * trail_width, trail_width, 1)
    weight_high, weight_low = split_weights(weights_own)
    segment = lax.all_gather(panel_own, "col", axis=0, tiled=True)
    trail_residual = (
        trail_own.astype(jnp.float32)
        - contract_cols(weight_high, segment)
        - contract_cols(weight_low, segment)
    )
    cross_factor = coupling_own.T
    return (panel_factor, cross_factor, trail_residual)


def solution(mesh):
    return jax.shard_map(
        per_device,
        mesh=mesh,
        in_specs=(
            P(("row", "col"), None),
            P(None, None, ("row", "col"), None),
            P("col", None),
            P("col", None),
            P(("row", "col"), None),
            P(("row", "col"), None),
            P(("row", "col"), None, None),
        ),
        out_specs=(P(), P("col", None), P("col", "row")),
        check_vma=False,
    )
```

profile of v0, /device:TPU:1, one launch (start us, length us, event | category | flops | bytes accessed | tf_op | source)
XLA Modules:
  0.0 593.3 jit_solution(4389010923176962485)
XLA Ops:
  7.2 1.8 pad_maximum_fusion
  9.2 0.8 select_reduce_fusion.4
  11.2 1.1 compare_and_fusion
  13.4 0.7 fusion.65
  14.9 55.6 %all-gather.3.cloned.1.call-done = bf16[2560,1024]{1,0:T(8,128)(2,1)} async-done(((bf16[160,1024]{1,0:T(8,128)(2,1)}), bf16[2560,1024]{1,0:T(8,128)(2,1)}) %all-gather.3.cloned.1.call-update) | async-done | bytes 5242896 | tf_op jit(solution)/shard_map/all_gather | solution.py:113
  70.5 5.5 multiply_reduce_fusion.1
  75.9 7.7 %gather_fusion = f32[512,2560]{1,0:T(8,128)} fusion(f32[2560,128]{0,1:T(8,128)} %get-tuple-element.64, s32[1024]{0:T(1024)S(1)} %pad_clamp_fusion.1), kind=kCustom, calls=%fused_computation | custom fusion | bytes 10487808 | tf_op jit(solution)/shard_map/jit(_take)/gather | solution.py:28
  83.6 7.1 %gather.17 = f32[2560,8,16,4]{0,3,2,1:T(4,128)} reshape(f32[2560,512]{0,1:T(8,128)} %bitcast.121) | data formatting | bytes 10485760 | tf_op jit(solution)/shard_map/jit(_take)/gather | solution.py:28
  90.7 4.6 fusion.1
  95.4 12.1 %multiply_reduce_fusion = f32[2560,3,8,16]{0,3,2,1:T(8,128)S(1)} fusion(f32[2560,4,8,16]{0,3,2,1:T(8,128)S(1)} %fusion.1, bf16[3,4,8,16,1024]{4,3,2,1,0:T(8,128)(2,1)S(1)} %bitcast.117, bf16[2560,1024]{1,0:T(8,128)(2,1)} %all-gather.3.cloned.1.call-done), kind=kOutput, calls=%fused_computation.4 | convolution fusion | flops 8059944960 | bytes 17563648 | tf_op jit(solution)/shard_map/dot_general | solution.py:17
  108.0 1.1 copy.66
  109.8 0.8 maximum_maximum_fusion
  110.6 2.2 gather_fusion.1
  112.8 8.5 %gather.19 = bf16[16,160,8,64]{1,0,3,2:T(8,128)(2,1)} reshape(bf16[2560,8,64]{0,2,1:T(8,128)(2,1)} %bitcast.120) | data formatting | bytes 5242880 | tf_op jit(solution)/shard_map/jit(_take)/gather | solution.py:40
  121.2 3.6 copy_select_fusion.1
  124.9 2.0 copy-done.5
  127.4 0.9 copy.69
  128.9 21.1 %all_to_all.10 = bf16[128,2,1024]{2,1,0:T(2,128)(2,1)S(1)} all-to-all(bf16[128,2,1024]{2,1,0:T(2,128)(2,1)S(1)} %reshape.290), channel_id=1, replica_groups=mesh['row'=8,'col'=16] {'row','col'}, dimensions={0} | all-to-all | bytes 1048576 | tf_op jit(solution)/shard_map/all_to_all | solution.py:124
  151.3 1.6 reshape.250
  152.9 4.3 slice.149
  157.3 4.8 all-to-all-start.1
  162.2 36.1 %all-to-all-done.1 = bf16[128,128,64]{1,2,0:T(8,128)(2,1)S(1)} async-done(((bf16[128,128,64]{1,2,0:T(8,128)(2,1)}), bf16[128,128,64]{1,2,0:T(8,128)(2,1)S(1)}, u32[]{:S(2)}, u32[]{:S(2)}) %all-to-all-start.1) | async-done | bytes 2097184 | tf_op jit(solution)/shard_map/all_to_all | solution.py:131
  198.3 1.6 copy.80
  199.9 40.1 %all-gather.5.cloned.1.call-done = bf16[512,8192]{1,0:T(8,128)(2,1)} async-done(((bf16[32,8192]{1,0:T(8,128)(2,1)}), bf16[512,8192]{1,0:T(8,128)(2,1)}) %all-gather.5.cloned.1.call-update) | async-done | bytes 8388624 | tf_op jit(solution)/shard_map/all_gather | solution.py:141
  240.1 6.1 %convolution_dynamic-update-slice_fusion.3 = f32[512,512]{0,1:T(8,128)S(1)} fusion(f32[512,512]{0,1:T(8,128)S(1)} %broadcast_in_dim.40, s32[]{:T(128)S(6)} %select_n.80, bf16[512,8192]{1,0:T(8,128)(2,1)} %all-gather.5.cloned.1.call-done, bf16[32,8192]{1,0:T(8,128)(2,1)S(1)} %copy-done.8), kind=kOutput, calls=%fused_computation.54 | convolution fusion | flops 268435456 | bytes 8978436 | tf_op jit(solution)/shard_map/dot_general | solution.py:69
  246.3 1.0 copy-done.11
  247.2 2.5 broadcast_in_dim.46
  249.8 3.1 convolution_dynamic-update-slice_fusion
  252.9 3.4 copy.81
  256.2 152.8 %all-reduce.4.cloned.1.call-done = (f32[512,512]{0,1:T(8,128)}, f32[512,2048]{1,0:T(8,128)}) async-done(((f32[512,512]{0,1:T(8,128)}, f32[512,2048]{1,0:T(8,128)}), (f32[512,512]{0,1:T(8,128)}, f32[512,2048]{1,0:T(8,128)})) %all-reduce.4.cloned.1.call-update) | async-done | bytes 5242896 | tf_op jit(solution)/shard_map/psum | solution.py:65
  409.0 1.4 select_add_fusion
  411.1 11.7 %cholesky.103 = f32[128,128]{1,0:T(8,128)S(1)} custom-call(f32[128,128]{1,0:T(8,128)S(1)} %cholesky.263), custom_call_target="Cholesky" | custom-call | tf_op jit(solution)/shard_map/jit(cholesky)/cholesky | solution.py:47
  423.0 9.8 %custom-call.32 = f32[1,128,128]{1,2,0:T(8,128)S(1)} custom-call(f32[1,128,128]{2,1,0:T(8,128)S(1)} %get-tuple-element.62), custom_call_target="InvertDiagBlocksLowerTriangular" | custom-call | tf_op jit(solution)/shard_map/jit(cholesky)/cholesky | solution.py:47
  433.6 11.7 %cholesky.215 = f32[128,128]{1,0:T(8,128)S(1)} custom-call(f32[128,128]{1,0:T(8,128)S(1)} %cholesky.267), custom_call_target="Cholesky" | custom-call | tf_op jit(solution)/shard_map/jit(cholesky)/cholesky | solution.py:47
  445.6 10.0 %custom-call.33 = f32[1,128,128]{1,2,0:T(8,128)S(1)} custom-call(f32[1,128,128]{2,1,0:T(8,128)S(1)} %get-tuple-element.60), custom_call_target="InvertDiagBlocksLowerTriangular" | custom-call | tf_op jit(solution)/shard_map/jit(cholesky)/cholesky | solution.py:47
  456.5 11.7 %cholesky.236 = f32[128,128]{1,0:T(8,128)S(1)} custom-call(f32[128,128]{1,0:T(8,128)S(1)} %cholesky.272), custom_call_target="Cholesky" | custom-call | tf_op jit(solution)/shard_map/jit(cholesky)/cholesky | solution.py:47
  468.4 9.8 %custom-call.34 = f32[1,128,128]{1,2,0:T(8,128)S(1)} custom-call(f32[1,128,128]{2,1,0:T(8,128)S(1)} %get-tuple-element.58), custom_call_target="InvertDiagBlocksLowerTriangular" | custom-call | tf_op jit(solution)/shard_map/jit(cholesky)/cholesky | solution.py:47
  479.0 11.9 %cholesky.253 = f32[128,128]{1,0:T(8,128)S(1)} custom-call(f32[128,128]{1,0:T(8,128)S(1)} %convolution_subtract_fusion.8), custom_call_target="Cholesky" | custom-call | tf_op jit(solution)/shard_map/jit(cholesky)/cholesky | solution.py:47
  493.7 4.8 broadcast_multiply_fusion
  501.1 1.2 fusion.30
  502.3 11.1 %while.1 = (s32[]{:T(128)}, f32[512,512]{0,1:T(8,128)S(1)}, s32[4,2]{0,1:T(2,128)S(1)}, f32[4,128,128]{2,1,0:T(8,128)}, s32[]{:T(128)}) while((s32[]{:T(128)}, f32[512,512]{0,1:T(8,128)S(1)}, s32[4,2]{0,1:T(2,128)S(1)}, f32[4,128,128]{2,1,0:T(8,128)}, s32[]{:T(128)}) %tuple.40), condition=%wide.while_cond, body=%wide.while_body.sunk | while | flops 2 | bytes 393329 | solution.py:48
  503.0 1.4 dynamic-slice.7
  505.8 1.4 dynamic-slice.7
  508.6 1.4 dynamic-slice.7
  511.4 1.4 dynamic-slice.7
  513.5 40.2 %custom-call.35 = f32[4,128,128]{1,2,0:T(8,128)S(1)} custom-call(f32[4,128,128]{2,1,0:T(8,128)} %get-tuple-element.10), custom_call_target="InvertDiagBlocksLowerTriangular" | custom-call | tf_op jit(solution)/shard_map/triangular_solve | solution.py:48
  553.7 2.4 fusion.27
  556.1 2.3 convolution_subtract_fusion.5
  558.4 1.1 fusion.58
  559.5 1.3 convolution_subtract_fusion.3
  560.7 1.1 fusion.60
  561.8 3.2 fusion.17
  565.0 1.0 fusion.62
  566.1 0.7 fusion.39
  566.8 1.0 fusion.61
  567.8 1.8 copy.82
  569.6 2.3 convolution_subtract_fusion.4
  571.9 1.0 fusion.59
  572.9 2.6 convolution_subtract_fusion.2
  575.5 1.0 fusion.57
  576.5 3.1 fusion.14
  579.7 1.0 fusion.56
  581.2 1.4 convolution_subtract_fusion.1
  582.7 3.6 convolution_subtract_fusion
  (103 shorter events, 19.5 us)
Async XLA Ops:
  7.2 88.2 %copy-start = (bf16[3,4,128,1024]{3,2,1,0:T(8,128)(2,1)S(1)}, bf16[3,4,128,1024]{3,2,1,0:T(8,128)(2,1)}, u32[]{:S(2)}) copy-start(bf16[3,4,128,1024]{3,2,1,0:T(8,128)(2,1)} %param.8) | copy-start | bytes 9437188
  7.2 63.3 %all-gather.3.cloned.1.call-start = ((), (), s32[]{:S(2)}) async-start(), calls=%async_computation.2 | async-start | bytes 5570560 | tf_op jit(solution)/shard_map/all_gather | solution.py:113
  9.1 230.9 %all-gather.5.cloned.1.call-start = ((), (), s32[]{:S(2)}) async-start(), calls=%async_computation.3 | async-start | bytes 8912896 | tf_op jit(solution)/shard_map/all_gather | solution.py:141
  124.9 2.0 copy-start.5
  157.3 82.8 %copy-start.8 = (bf16[32,8192]{1,0:T(8,128)(2,1)S(1)}, bf16[32,8192]{1,0:T(8,128)(2,1)}, u32[]{:S(2)}) copy-start(bf16[32,8192]{1,0:T(8,128)(2,1)} %reshape.250) | copy-start | bytes 1572868
  157.3 41.0 %all-to-all-start.1 = ((bf16[128,128,64]{1,2,0:T(8,128)(2,1)}), bf16[128,128,64]{1,2,0:T(8,128)(2,1)S(1)}, u32[]{:S(2)}, u32[]{:S(2)}) async-start(bf16[128,128,64]{1,2,0:T(8,128)(2,1)} %bitcast.123), calls=%async_computation.1 | async-start | bytes 4194304 | tf_op jit(solution)/shard_map/all_to_all | solution.py:131
  162.1 246.9 %all-reduce.4.cloned.1.call-start = ((), (), s32[]{:S(2)}) async-start(), calls=%async_computation.4 | async-start | bytes 10485760 | tf_op jit(solution)/shard_map/psum | solution.py:65
  240.1 9.7 %copy-start.2 = (bf16[512,8192]{1,0:T(8,128)(2,1)S(1)}, bf16[512,8192]{1,0:T(8,128)(2,1)}, u32[]{:S(2)}) copy-start(bf16[512,8192]{1,0:T(8,128)(2,1)} %all-gather.5.cloned.1.call-done) | copy-start | bytes 25165828
  246.2 1.0 copy-start.11
  247.2 2.5 copy-start.7
  409.0 1.8 copy-start.10
  513.5 45.9 %copy-start.9 = (f32[512,512]{0,1:T(8,128)}, f32[512,512]{0,1:T(8,128)S(1)}, u32[]{:S(2)}) copy-start(f32[512,512]{0,1:T(8,128)S(1)} %get-tuple-element.126) | copy-start | bytes 3145732
  553.7 5.8 copy-start.4
  561.8 4.3 copy-start.3
  572.9 7.8 %slice-start = ((s8[8388608]{0:T(1024)(128)(4,1)}), s8[4194304]{0:T(1024)(128)(4,1)S(1)}, s32[]{:S(2)}) async-start(s8[8388608]{0:T(1024)(128)(4,1)} %bitcast.118), calls=%async_computation.5 | async-start | bytes 8388608
  576.5 4.2 slice-start.1
  579.6 1.6 copy-start.6
  582.7 3.6 copy-start.1
Sparse Core Ops, SparseCore 0:
  10.8 59.6 all-gather.2
  153.0 86.8 all-gather.4
  253.0 156.0 all-reduce.3
where the time goes:
time: 604 us; the launch traced here: 593 us
  waiting for transfers between devices  285 us (47%)
  other arithmetic  145 us (24%)
  local copies, waits for them, and re-layouts  61.7 us (10%)
  matrix products  58.4 us (10%)
  blocking collectives  21.1 us (3%)
  between operations  17.4 us (3%)
    psum x1, waiting for transfers between devices, reduce_products(): return lax.psum((gram_part, cross_part), ('row', 'col'))  153 us
    another operation x15, other arithmetic, factor_panel(): lower_factor = jnp.linalg.cholesky(gram_matrix)  79.5 us
    all_gather x1, waiting for transfers between devices, per_device(): lax.all_gather(own_envs, 'col', axis=0, tiled=True)  55.6 us
    another operation x3, other arithmetic, factor_panel(): lax.linalg.triangular_solve(lower_factor, cross_sum / total_rows, left_si...  41.4 us
    all_gather x1, waiting for transfers between devices, per_device(): segment = lax.all_gather(panel_own, 'col', axis=0, tiled=True)  40.1 us
    all_to_all x1, waiting for transfers between devices, per_device(): lax.all_to_all(arrange_direct(trail_rows, row_count, col_count), ('row',...  36.1 us
    all_to_all x1, blocking collectives, per_device(): lax.all_to_all(arrange_direct(panel_rows, row_count, col_count), ('row',...  21.1 us
    gather x2, local copies, waits for them, and re-layouts, slot_rows(): jnp.take(correlation, flat_index, axis=1)  14.8 us
  transfers between devices with their start and end apart: 4, of which 4 were waited for; matrix products, arithmetic and copies ran while one was open for 3% of the time, Pallas kernels for 0%

commit v1 on v0

--- a/solution.py
+++ b/solution.py
@@ -110,7 +110,9 @@
     total_rows = row_count * row_count * col_count * slot_count
     own_envs = jnp.concatenate([sparse_panel, sparse_trail], axis=0)
     kernel_rows = slot_rows(
-        lax.all_gather(own_envs, "col", axis=0, tiled=True),
+        jnp.concatenate(
+            lax.all_to_all(jnp.stack([own_envs] * lax.axis_size("col")), "col", 0, 0), axis=0
+        ),
         descriptors,
         slope_here,
         count_here,

time: 604 us -> 634 us (1.050); the launches traced: 593 us -> 630 us
  waiting for transfers between devices: 285 us -> 305 us
  blocking collectives: 21.1 us -> 30.1 us
  starting transfers between devices: 4.96 us -> 13.5 us
    all_to_all x0 -> x1, waiting for transfers between devices: none -> 76.3 us  [per_device(): lax.all_to_all(jnp.stack([own_envs] * lax.axis_size('col')), 'col', 0, 0)]
    all_gather x1 -> x0, waiting for transfers between devices: 55.6 us -> none  [per_device(): lax.all_gather(own_envs, 'col', axis=0, tiled=True)]
    all_to_all x1, blocking collectives: 21.1 us -> 30.1 us  [per_device(): lax.all_to_all(arrange_direct(panel_rows, row_count, col_count), ('row',...]
    all_to_all x0 -> x1, starting transfers between devices: none -> 8.62 us  [per_device(): lax.all_to_all(jnp.stack([own_envs] * lax.axis_size('col')), 'col', 0, 0)]
    another operation x20 -> x21, local copies, waits for them, and re-layouts: 11.1 us -> 14.1 us
  transfers between devices with their start and end apart: 4 -> 4, of which waited for: 4 -> 4; matrix products, arithmetic and copies ran while one was open for 3% -> 2% of each run, Pallas kernels for 0% -> 0%
where the time goes in v1:
time: 634 us; the launch traced here: 630 us
  waiting for transfers between devices  305 us (48%)
  other arithmetic  140 us (22%)
  local copies, waits for them, and re-layouts  64.9 us (10%)
  matrix products  58.4 us (9%)
  blocking collectives  30.1 us (5%)
  between operations  17.6 us (3%)
  starting transfers between devices  13.5 us (2%)
    psum x1, waiting for transfers between devices, reduce_products(): return lax.psum((gram_part, cross_part), ('row', 'col'))  153 us
    another operation x15, other arithmetic, factor_panel(): lower_factor = jnp.linalg.cholesky(gram_matrix)  79.7 us
    all_to_all x1, waiting for transfers between devices, per_device(): lax.all_to_all(jnp.stack([own_envs] * lax.axis_size('col')), 'col', 0, 0)  76.3 us
    another operation x3, other arithmetic, factor_panel(): lax.linalg.triangular_solve(lower_factor, cross_sum / total_rows, left_si...  41.4 us
    all_gather x1, waiting for transfers between devices, per_device(): segment = lax.all_gather(panel_own, 'col', axis=0, tiled=True)  40.1 us
    all_to_all x1, waiting for transfers between devices, per_device(): lax.all_to_all(arrange_direct(trail_rows, row_count, col_count), ('row',...  36.1 us
    all_to_all x1, blocking collectives, per_device(): lax.all_to_all(arrange_direct(panel_rows, row_count, col_count), ('row',...  30.1 us
    gather x2, local copies, waits for them, and re-layouts, slot_rows(): jnp.take(correlation, flat_index, axis=1)  15 us
  transfers between devices with their start and end apart: 4, of which 4 were waited for; matrix products, arithmetic and copies ran while one was open for 2% of the time, Pallas kernels for 0%

profile of v1, /device:TPU:1, one launch (start us, length us, event | category | flops | bytes accessed | tf_op | source)
XLA Modules:
  0.0 629.7 jit_solution(16844791477071226365)
XLA Ops:
  7.2 1.1 pad_maximum_fusion
  8.3 3.0 stack.2
  11.3 8.6 %all-to-all-start = ((bf16[16,160,1024]{2,1,0:T(8,128)(2,1)}), bf16[16,160,1024]{2,1,0:T(8,128)(2,1)}, u32[]{:S(2)}, u32[]{:S(2)}) async-start(bf16[16,160,1024]{2,1,0:T(8,128)(2,1)} %stack.2), calls=%async_computation | async-start | bytes 10485760 | tf_op jit(solution)/shard_map/all_to_all | solution.py:114
  21.1 76.3 %all-to-all-done = bf16[16,160,1024]{2,1,0:T(8,128)(2,1)} async-done(((bf16[16,160,1024]{2,1,0:T(8,128)(2,1)}), bf16[16,160,1024]{2,1,0:T(8,128)(2,1)}, u32[]{:S(2)}, u32[]{:S(2)}) %all-to-all-start) | async-done | bytes 5242912 | tf_op jit(solution)/shard_map/all_to_all | solution.py:114
  97.4 5.4 multiply_reduce_fusion.1
  102.8 7.8 %gather_fusion = f32[512,2560]{1,0:T(8,128)} fusion(f32[2560,128]{0,1:T(8,128)} %get-tuple-element.64, s32[1024]{0:T(1024)S(1)} %pad_clamp_fusion.1), kind=kCustom, calls=%fused_computation | custom fusion | bytes 10487808 | tf_op jit(solution)/shard_map/jit(_take)/gather | solution.py:28
  110.7 7.1 %gather.17 = f32[2560,8,16,4]{0,3,2,1:T(4,128)} reshape(f32[2560,512]{0,1:T(8,128)} %bitcast.122) | data formatting | bytes 10485760 | tf_op jit(solution)/shard_map/jit(_take)/gather | solution.py:28
  117.8 4.6 fusion
  122.4 12.1 %multiply_reduce_fusion = f32[2560,3,8,16]{0,3,2,1:T(8,128)S(1)} fusion(f32[2560,4,8,16]{0,3,2,1:T(8,128)S(1)} %fusion, bf16[2560,1024,1,1,1]{1,0,4,3,2:T(8,128)(2,1)} %bitcast.9, bf16[3,4,8,16,1024]{4,3,2,1,0:T(8,128)(2,1)S(1)} %bitcast.118), kind=kOutput, calls=%fused_computation.4 | convolution fusion | flops 8059944960 | bytes 17563648 | tf_op jit(solution)/shard_map/dot_general | solution.py:17
  135.0 1.1 copy.66
  136.8 0.8 maximum_maximum_fusion
  137.6 2.2 gather_fusion.1
  139.9 8.7 %gather.19 = bf16[16,160,8,64]{1,0,3,2:T(8,128)(2,1)} reshape(bf16[2560,8,64]{0,2,1:T(8,128)(2,1)} %bitcast.121) | data formatting | bytes 5242880 | tf_op jit(solution)/shard_map/jit(_take)/gather | solution.py:40
  148.5 3.6 copy_select_fusion.1
  152.2 2.0 copy-done.5
  154.7 0.9 copy.69
  156.2 30.1 %all_to_all.15 = bf16[128,2,1024]{2,1,0:T(2,128)(2,1)S(1)} all-to-all(bf16[128,2,1024]{2,1,0:T(2,128)(2,1)S(1)} %reshape.296), channel_id=1, replica_groups=mesh['row'=8,'col'=16] {'row','col'}, dimensions={0} | all-to-all | bytes 1048576 | tf_op jit(solution)/shard_map/all_to_all | solution.py:126
  187.6 1.6 reshape.256
  189.3 4.3 slice.149
  193.6 4.8 all-to-all-start.2
  198.5 36.1 %all-to-all-done.2 = bf16[128,128,64]{1,2,0:T(8,128)(2,1)S(1)} async-done(((bf16[128,128,64]{1,2,0:T(8,128)(2,1)}), bf16[128,128,64]{1,2,0:T(8,128)(2,1)S(1)}, u32[]{:S(2)}, u32[]{:S(2)}) %all-to-all-start.2) | async-done | bytes 2097184 | tf_op jit(solution)/shard_map/all_to_all | solution.py:133
  234.7 1.6 copy.80
  236.3 40.1 %all-gather.2.cloned.1.call-done = bf16[512,8192]{1,0:T(8,128)(2,1)} async-done(((bf16[32,8192]{1,0:T(8,128)(2,1)}), bf16[512,8192]{1,0:T(8,128)(2,1)}) %all-gather.2.cloned.1.call-update) | async-done | bytes 8388624 | tf_op jit(solution)/shard_map/all_gather | solution.py:143
  276.5 6.1 convolution_dynamic-update-slice_fusion.3
  282.6 1.0 copy-done.11
  283.6 2.5 broadcast_in_dim.46
  286.1 3.1 convolution_dynamic-update-slice_fusion
  289.2 3.1 copy.81
  292.3 152.9 %all-reduce.4.cloned.1.call-done = (f32[512,512]{0,1:T(8,128)}, f32[512,2048]{1,0:T(8,128)}) async-done(((f32[512,512]{0,1:T(8,128)}, f32[512,2048]{1,0:T(8,128)}), (f32[512,512]{0,1:T(8,128)}, f32[512,2048]{1,0:T(8,128)})) %all-reduce.4.cloned.1.call-update) | async-done | bytes 5242896 | tf_op jit(solution)/shard_map/psum | solution.py:65
  445.2 1.4 select_add_fusion
  447.2 11.7 %cholesky.103 = f32[128,128]{1,0:T(8,128)S(1)} custom-call(f32[128,128]{1,0:T(8,128)S(1)} %cholesky.263), custom_call_target="Cholesky" | custom-call | tf_op jit(solution)/shard_map/jit(cholesky)/cholesky | solution.py:47
  459.1 9.8 %custom-call.32 = f32[1,128,128]{1,2,0:T(8,128)S(1)} custom-call(f32[1,128,128]{2,1,0:T(8,128)S(1)} %get-tuple-element.62), custom_call_target="InvertDiagBlocksLowerTriangular" | custom-call | tf_op jit(solution)/shard_map/jit(cholesky)/cholesky | solution.py:47
  469.7 11.7 %cholesky.215 = f32[128,128]{1,0:T(8,128)S(1)} custom-call(f32[128,128]{1,0:T(8,128)S(1)} %cholesky.267), custom_call_target="Cholesky" | custom-call | tf_op jit(solution)/shard_map/jit(cholesky)/cholesky | solution.py:47
  481.7 10.2 %custom-call.33 = f32[1,128,128]{1,2,0:T(8,128)S(1)} custom-call(f32[1,128,128]{2,1,0:T(8,128)S(1)} %get-tuple-element.60), custom_call_target="InvertDiagBlocksLowerTriangular" | custom-call | tf_op jit(solution)/shard_map/jit(cholesky)/cholesky | solution.py:47
  492.9 11.7 %cholesky.236 = f32[128,128]{1,0:T(8,128)S(1)} custom-call(f32[128,128]{1,0:T(8,128)S(1)} %cholesky.272), custom_call_target="Cholesky" | custom-call | tf_op jit(solution)/shard_map/jit(cholesky)/cholesky | solution.py:47
  504.7 9.8 %custom-call.34 = f32[1,128,128]{1,2,0:T(8,128)S(1)} custom-call(f32[1,128,128]{2,1,0:T(8,128)S(1)} %get-tuple-element.58), custom_call_target="InvertDiagBlocksLowerTriangular" | custom-call | tf_op jit(solution)/shard_map/jit(cholesky)/cholesky | solution.py:47
  515.3 11.9 %cholesky.253 = f32[128,128]{1,0:T(8,128)S(1)} custom-call(f32[128,128]{1,0:T(8,128)S(1)} %convolution_subtract_fusion.8), custom_call_target="Cholesky" | custom-call | tf_op jit(solution)/shard_map/jit(cholesky)/cholesky | solution.py:47
  528.6 0.7 compare_reduce_fusion.1
  530.1 4.8 broadcast_multiply_fusion
  537.5 1.2 fusion.29
  538.7 11.2 %while.1 = (s32[]{:T(128)}, f32[512,512]{0,1:T(8,128)S(1)}, s32[4,2]{0,1:T(2,128)S(1)}, f32[4,128,128]{2,1,0:T(8,128)}, s32[]{:T(128)}) while((s32[]{:T(128)}, f32[512,512]{0,1:T(8,128)S(1)}, s32[4,2]{0,1:T(2,128)S(1)}, f32[4,128,128]{2,1,0:T(8,128)}, s32[]{:T(128)}) %tuple.40), condition=%wide.while_cond, body=%wide.while_body.sunk | while | flops 2 | bytes 393329 | solution.py:48
  539.4 1.4 dynamic-slice.7
  542.2 1.4 dynamic-slice.7
  545.0 1.4 dynamic-slice.7
  547.8 1.4 dynamic-slice.7
  549.9 40.2 %custom-call.35 = f32[4,128,128]{1,2,0:T(8,128)S(1)} custom-call(f32[4,128,128]{2,1,0:T(8,128)} %get-tuple-element.10), custom_call_target="InvertDiagBlocksLowerTriangular" | custom-call | tf_op jit(solution)/shard_map/triangular_solve | solution.py:48
  590.1 2.4 fusion.26
  592.5 2.3 convolution_subtract_fusion.5
  594.8 1.1 fusion.57
  595.9 1.3 convolution_subtract_fusion.3
  597.2 1.1 fusion.59
  598.2 3.2 fusion.16
  601.4 1.0 fusion.61
  602.5 0.7 fusion.38
  603.2 1.0 fusion.60
  604.2 1.8 copy.82
  606.0 2.3 convolution_subtract_fusion.4
  608.3 1.0 fusion.58
  609.3 2.5 convolution_subtract_fusion.2
  611.9 1.0 fusion.56
  612.9 3.1 fusion.13
  616.0 1.0 fusion.55
  617.6 1.4 convolution_subtract_fusion.1
  619.1 3.6 convolution_subtract_fusion
  (111 shorter events, 16.7 us)
Async XLA Ops:
  7.2 115.2 %copy-start = (bf16[3,4,128,1024]{3,2,1,0:T(8,128)(2,1)S(1)}, bf16[3,4,128,1024]{3,2,1,0:T(8,128)(2,1)}, u32[]{:S(2)}) copy-start(bf16[3,4,128,1024]{3,2,1,0:T(8,128)(2,1)} %param.8) | copy-start | bytes 9437188
  11.3 8.7 %copy-start.15 = (s32[1,8]{1,0:T(1,128)S(1)}, s32[1,8]{1,0:T(1,128)}, u32[]{:S(2)}) copy-start(s32[1,8]{1,0:T(1,128)} %param.12) | copy-start | bytes 100
  11.3 8.8 %copy-start.14 = (s32[1,8]{1,0:T(1,128)S(1)}, s32[1,8]{1,0:T(1,128)}, u32[]{:S(2)}) copy-start(s32[1,8]{1,0:T(1,128)} %param.11) | copy-start | bytes 100
  11.3 8.8 %copy-start.13 = (s32[8,16,4]{1,2,0:T(4,128)S(1)}, s32[8,16,4]{1,2,0:T(4,128)}, u32[]{:S(2)}) copy-start(s32[8,16,4]{1,2,0:T(4,128)} %param.13) | copy-start | bytes 6148
  11.3 86.1 %copy-start.12 = (bf16[128,1024]{1,0:T(8,128)(2,1)S(1)}, bf16[128,1024]{1,0:T(8,128)(2,1)}, u32[]{:S(2)}) copy-start(bf16[128,1024]{1,0:T(8,128)(2,1)} %param.7) | copy-start | bytes 786436
  11.3 86.1 %all-to-all-start = ((bf16[16,160,1024]{2,1,0:T(8,128)(2,1)}), bf16[16,160,1024]{2,1,0:T(8,128)(2,1)}, u32[]{:S(2)}, u32[]{:S(2)}) async-start(bf16[16,160,1024]{2,1,0:T(8,128)(2,1)} %stack.2), calls=%async_computation | async-start | bytes 10485760 | tf_op jit(solution)/shard_map/all_to_all | solution.py:114
  19.9 256.4 %all-gather.2.cloned.1.call-start = ((), (), s32[]{:S(2)}) async-start(), calls=%async_computation.3 | async-start | bytes 8912896 | tf_op jit(solution)/shard_map/all_gather | solution.py:143
  152.2 2.0 copy-start.5
  193.6 82.8 %copy-start.8 = (bf16[32,8192]{1,0:T(8,128)(2,1)S(1)}, bf16[32,8192]{1,0:T(8,128)(2,1)}, u32[]{:S(2)}) copy-start(bf16[32,8192]{1,0:T(8,128)(2,1)} %reshape.256) | copy-start | bytes 1572868
  193.6 41.0 %all-to-all-start.2 = ((bf16[128,128,64]{1,2,0:T(8,128)(2,1)}), bf16[128,128,64]{1,2,0:T(8,128)(2,1)S(1)}, u32[]{:S(2)}, u32[]{:S(2)}) async-start(bf16[128,128,64]{1,2,0:T(8,128)(2,1)} %bitcast.124), calls=%async_computation.2 | async-start | bytes 4194304 | tf_op jit(solution)/shard_map/all_to_all | solution.py:133
  198.5 246.7 %all-reduce.4.cloned.1.call-start = ((), (), s32[]{:S(2)}) async-start(), calls=%async_computation.4 | async-start | bytes 10485760 | tf_op jit(solution)/shard_map/psum | solution.py:65
  276.5 9.7 %copy-start.2 = (bf16[512,8192]{1,0:T(8,128)(2,1)S(1)}, bf16[512,8192]{1,0:T(8,128)(2,1)}, u32[]{:S(2)}) copy-start(bf16[512,8192]{1,0:T(8,128)(2,1)} %all-gather.2.cloned.1.call-done) | copy-start | bytes 25165828
  282.6 1.0 copy-start.11
  283.6 2.5 copy-start.7
  445.2 1.8 copy-start.10
  549.9 46.0 %copy-start.9 = (f32[512,512]{0,1:T(8,128)}, f32[512,512]{0,1:T(8,128)S(1)}, u32[]{:S(2)}) copy-start(f32[512,512]{0,1:T(8,128)S(1)} %get-tuple-element.126) | copy-start | bytes 3145732
  590.1 5.8 copy-start.4
  598.2 4.3 copy-start.3
  609.3 7.8 %slice-start = ((s8[8388608]{0:T(1024)(128)(4,1)}), s8[4194304]{0:T(1024)(128)(4,1)S(1)}, s32[]{:S(2)}) async-start(s8[8388608]{0:T(1024)(128)(4,1)} %bitcast.119), calls=%async_computation.5 | async-start | bytes 8388608
  612.9 4.2 slice-start.1
  616.0 1.6 copy-start.6
  619.1 3.6 copy-start.1
Sparse Core Ops, SparseCore 0:
  189.4 86.8 all-gather.1
  289.3 155.8 all-reduce.3
